TPU v7x, 512 devices: a whole 4x8x8 slice. The times are simulated.
512 devices in a mesh: dp: 32 (over x, y), region: 16 (over z, core).
Axes of the slice: x: 4, y: 8, z: 8, core: 2. Of those that a mesh axis runs over, the one named last changes fastest.
Arguments:
- inputs: bfloat16 [32, 2, 4096, 256], P('dp', None, 'region'), may hold values from -6 to 6
- cotangent: bfloat16 [32, 2, 4096, 256], P('dp', None, 'region'), may hold values from -6 to 6
- w_filter: bfloat16 [2, 256, 256], replicated, may hold values from -0.25 to 0.25
- w_gate: bfloat16 [2, 256, 256], replicated, may hold values from -0.25 to 0.25
- w_mix: bfloat16 [2, 256, 256], replicated, may hold values from -0.25 to 0.25
- neighbours: int32 [32, 6], replicated, may hold values from 0 to 31, as said below
- adjacency: bfloat16 [32, 6, 128, 128], P('region'), may hold values from -0.21875 to 0.21875
Outputs:
- grad_inputs: bfloat16 [32, 2, 4096, 256], P('dp', None, 'region')
- grad_filter: float32 [2, 256, 256], replicated
- grad_gate: float32 [2, 256, 256], replicated
- grad_mix: float32 [2, 256, 256], replicated
Inputs may be any that keep to these rules, and one draw needn't show every extreme that they name: `neighbours`: for every region r (tiles r * 2 to (r + 1) * 2 - 1), exactly 11 of the 12 entries of its tiles' lists name tiles of other regions, each of a different region, so at most 1 name tiles of any one other region; all other entries name tiles of region r.
All inputs are finite; a program needn't handle non-finite values.
Results may differ from a plain program's by a relative error of at most 0.0053.
Values may be sent and summed in bfloat16 or wider, within the bound.
A program may use at most 64 MiB of HBM per device.

v0:
```python
import math
import jax
import jax.numpy as jnp
from jax import lax
from jax.sharding import PartitionSpec as P

CAP = 1


def per_device(inputs, cotangent, w_filter, w_gate, w_mix, neighbours, adjacency):
    regions = lax.axis_size("region")
    region_id = lax.axis_index("region")
    windows, steps, site_count, chans = inputs.shape
    tiles_dev = site_count // 128
    per_tile = neighbours.shape[1]
    entries = tiles_dev * per_tile
    capacity = CAP
    table = neighbours.reshape(regions, entries)
    owners = table // tiles_dev
    local_tile = table % tiles_dev
    sources = jnp.arange(regions, dtype=jnp.int32)
    positions = jnp.arange(entries)
    earlier = positions[:, None] > positions[None, :]
    ranks = jnp.sum(
        ((owners[:, :, None] == owners[:, None, :]) & earlier[None]).astype(jnp.int32), axis=2
    )
    slot_ids = jnp.arange(capacity)
    remote_entry = owners != sources[:, None]
    hits = (
        (owners[:, None, :] == region_id)
        & (ranks[:, None, :] == slot_ids[None, :, None])
        & remote_entry[:, None, :]
    )
    send_tile = jnp.sum(jnp.where(hits, local_tile[:, None, :], 0), axis=2).reshape(-1)
    send_used = jnp.any(hits, axis=2).reshape(-1)
    own_owner = lax.dynamic_index_in_dim(owners, region_id, 0, keepdims=False)
    own_rank = lax.dynamic_index_in_dim(ranks, region_id, 0, keepdims=False)
    own_tiles = lax.dynamic_index_in_dim(table, region_id, 0, keepdims=False)
    own_local_tile = lax.dynamic_index_in_dim(local_tile, region_id, 0, keepdims=False)
    at_home = own_owner == region_id
    drop_index = jnp.where(at_home, regions * capacity, own_owner * capacity + own_rank)
    w_cat = jnp.concatenate(
        [
            jnp.concatenate([w_filter[0], w_gate[0]], axis=1),
            jnp.concatenate([w_filter[1], w_gate[1]], axis=1),
        ],
        axis=0,
    )
    w_mixed = w_mix.reshape(2 * chans, chans)
    previous = jnp.concatenate([jnp.zeros_like(inputs[:, :1]), inputs[:, :-1]], axis=1)
    joint = jnp.concatenate([inputs, previous], axis=3)
    act = jnp.einsum("btsi,io->btso", joint, w_cat, preferred_element_type=jnp.float32)
    filt = jnp.tanh(act[..., :chans])
    gate = jax.nn.sigmoid(act[..., chans:])
    hidden = (filt * gate).astype(jnp.bfloat16)
    tiled = hidden.reshape(windows, steps, tiles_dev, 128, chans)
    piece = lax.all_gather(tiled, "region", axis=2, tiled=True)
    count = piece.shape[2]
    select = (own_tiles[:, None] == jnp.arange(count)[None, :]).astype(jnp.bfloat16)
    chosen = jnp.einsum("en,btnqc->bteqc", select, piece, preferred_element_type=jnp.float32)
    chosen = chosen.astype(jnp.bfloat16).reshape(windows, steps, tiles_dev, per_tile, 128, chans)
    graph_sum = jnp.einsum(
        "jkpq,btjkqc->btjpc", adjacency, chosen, preferred_element_type=jnp.float32
    )
    graph = graph_sum.astype(jnp.bfloat16).reshape(windows, steps, site_count, chans)
    both = jnp.concatenate([hidden, graph], axis=3)
    mix_sum = jnp.einsum("btsi,btsc->ic", both, cotangent, preferred_element_type=jnp.float32)
    back = jnp.einsum("btsc,ic->btsi", cotangent, w_mixed, preferred_element_type=jnp.float32)
    direct = back[..., :chans]
    graph_cot = (
        back[..., chans:].astype(jnp.bfloat16).reshape(windows, steps, tiles_dev, 128, chans)
    )
    term = jnp.einsum(
        "jkpq,btjpc->btjkqc", adjacency, graph_cot, preferred_element_type=jnp.float32
    )
    term = term.astype(jnp.bfloat16).reshape(windows, steps, entries, 128, chans)
    outgoing_back = jnp.zeros((windows, steps, regions * capacity, 128, chans), jnp.bfloat16)
    outgoing_back = outgoing_back.at[:, :, drop_index].set(term, mode="drop")
    outgoing_back = outgoing_back.reshape(windows, steps, regions, capacity, 128, chans)
    returned = lax.all_to_all(outgoing_back, "region", split_axis=2, concat_axis=2, tiled=True)
    returned = returned.reshape(windows, steps, regions * capacity, 128, chans)
    owner_hot = (
        (send_tile[None, :] == jnp.arange(tiles_dev)[:, None]) & send_used[None, :]
    ).astype(jnp.bfloat16)
    graph_grad = jnp.einsum(
        "ln,btnqc->btlqc", owner_hot, returned, preferred_element_type=jnp.float32
    )
    home_hot = (
        (own_local_tile[None, :] == jnp.arange(tiles_dev)[:, None]) & at_home[None, :]
    ).astype(jnp.bfloat16)
    home_grad = jnp.einsum("le,bteqc->btlqc", home_hot, term, preferred_element_type=jnp.float32)
    grad_hidden = direct + (graph_grad + home_grad).reshape(windows, steps, site_count, chans)
    act_cot = jnp.concatenate(
        [grad_hidden * gate * (1.0 - filt * filt), grad_hidden * filt * gate * (1.0 - gate)], axis=3
    ).astype(jnp.bfloat16)
    conv_sum = jnp.einsum("btsi,btso->io", joint, act_cot, preferred_element_type=jnp.float32)
    back_in = jnp.einsum("btso,io->btsi", act_cot, w_cat, preferred_element_type=jnp.float32)
    later = jnp.concatenate(
        [back_in[:, 1:, :, chans:], jnp.zeros((windows, 1, site_count, chans), jnp.float32)], axis=1
    )
    grad_inputs = (cotangent.astype(jnp.float32) + back_in[..., :chans] + later).astype(
        jnp.bfloat16
    )
    conv_total, mix_total = lax.psum((conv_sum, mix_sum), ("dp", "region"))
    total_rows = windows * lax.axis_size("dp") * steps * site_count * regions
    factor = 1.0 / math.sqrt(total_rows)
    grad_filter = (conv_total[:, :chans] * factor).reshape(2, chans, chans)
    grad_gate = (conv_total[:, chans:] * factor).reshape(2, chans, chans)
    grad_mix = (mix_total * factor).reshape(2, chans, chans)
    return (grad_inputs, grad_filter, grad_gate, grad_mix)


def solution(mesh):
    return jax.shard_map(
        per_device,
        mesh=mesh,
        in_specs=(
            P("dp", None, "region", None),
            P("dp", None, "region", None),
            P(),
            P(),
            P(),
            P(),
            P("region", None, None, None),
        ),
        out_specs=(P("dp", None, "region", None), P(), P(), P()),
        check_vma=False,
    )
```

profile of v0, /device:TPU:17, one launch (start us, length us, event | category | flops | bytes accessed | tf_op | source)
XLA Modules:
  0.0 429.3 jit_solution(3742528526093285278)
XLA Ops:
  7.2 0.0 copy-start
  7.2 0.8 copy.73
  8.0 0.1 reshape.354
  8.1 0.6 copy-done.15
  8.7 0.1 copy.74
  8.8 0.6 negate_select_fusion.4
  9.4 0.1 copy.78
  9.5 0.8 fusion.81
  10.2 0.4 convert_reduce_fusion
  10.6 0.2 select_reduce_fusion
  10.8 0.6 fusion.70
  11.4 1.4 convolution_bitcast_fusion
  12.8 0.9 copy-done.1
  13.7 0.6 fusion.12
  14.3 0.7 copy.80
  15.0 0.1 copy.81
  15.2 1.6 broadcast.246
  16.8 5.3 %scatter_fusion = bf16[2,16,128,256]{3,2,1,0:T(8,128)(2,1)} fusion(bf16[2,16,128,256]{3,2,1,0:T(8,128)(2,1)} %broadcast.246, s32[12]{0:T(128)} %fusion.70, bf16[12,2,128,256]{3,2,1,0:T(8,128)(2,1)S(1)} %copy.81), kind=kCustom, calls=%fused_computation | custom fusion | bytes 4718640 | tf_op jit(solution)/shard_map/scatter | solution.py:78
  22.0 3.1 copy.82
  25.2 11.1 %all-to-all-start = ((bf16[1,2,16,1,128,256]{5,4,1,3,0,2:T(8,128)(2,1)}), bf16[1,2,16,1,128,256]{5,4,1,3,0,2:T(8,128)(2,1)}, u32[]{:S(2)}, u32[]{:S(2)}) async-start(bf16[1,2,16,1,128,256]{5,4,1,3,0,2:T(8,128)(2,1)} %copy.82), calls=%async_computation | async-start | bytes 4194304 | tf_op jit(solution)/shard_map/all_to_all | solution.py:80
  36.3 0.0 all-gather.2.cloned.1.call-start
  36.4 0.1 reshape.359
  36.4 0.1 copy.85
  36.6 0.2 fusion.51
  36.9 0.6 copy-done.7
  37.5 1.4 convolution_bitcast_fusion.3
  38.9 46.4 %all-to-all-done = bf16[1,2,16,1,128,256]{5,4,1,3,0,2:T(8,128)(2,1)} async-done(((bf16[1,2,16,1,128,256]{5,4,1,3,0,2:T(8,128)(2,1)}), bf16[1,2,16,1,128,256]{5,4,1,3,0,2:T(8,128)(2,1)}, u32[]{:S(2)}, u32[]{:S(2)}) %all-to-all-start) | async-done | bytes 2097184 | tf_op jit(solution)/shard_map/all_to_all | solution.py:80
  85.4 2.9 fusion.3
  88.3 1.1 fusion.19
  89.4 0.1 copy-done.2
  89.5 0.3 fusion.42
  89.8 0.7 copy.92
  90.5 0.0 all-gather.2.cloned.1.call-update
  90.5 0.0 all-reduce.5.cloned.1.call-start
  90.6 0.7 fusion.69
  91.3 1.4 convolution_bitcast_fusion.1
  92.7 42.5 %all-gather.2.cloned.1.call-done = bf16[1,2,32,128,256]{4,3,1,0,2:T(8,128)(2,1)} async-done(((bf16[1,2,2,128,256]{4,3,1,0,2:T(8,128)(2,1)}), bf16[1,2,32,128,256]{4,3,1,0,2:T(8,128)(2,1)}) %all-gather.2.cloned.1.call-update) | async-done | bytes 4194320 | tf_op jit(solution)/shard_map/all_gather | solution.py:57
  135.2 4.7 %convert_bitcast_fusion = bf16[1,2,12,128,256]{4,2,3,1,0:T(8,128)(2,1)S(1)} fusion(bf16[1,2,32,128,256]{4,3,1,0,2:T(8,128)(2,1)} %all-gather.2.cloned.1.call-done, s32[12]{0:T(128)S(1)} %fusion.69), kind=kOutput, calls=%fused_computation.9 | convolution fusion | flops 51118464 | bytes 5767216 | tf_op jit(solution)/shard_map/en,btnqc->bteqc/dot_general | solution.py:60
  139.9 0.6 copy.94
  140.5 0.4 fusion.25
  140.9 0.5 copy-done.3
  141.4 1.1 convolution_bitcast_fusion.4
  142.6 0.0 all-reduce.5.cloned.1.call-update
  142.6 0.5 convolution_bitcast_fusion.2
  143.1 0.8 fusion.32
  143.9 275.5 %all-reduce.5.cloned.1.call-done = (f32[512,512]{1,0:T(8,128)}, f32[512,256]{1,0:T(8,128)}) async-done(((f32[512,512]{1,0:T(8,128)}, f32[512,256]{1,0:T(8,128)}), (f32[512,512]{1,0:T(8,128)}, f32[512,256]{1,0:T(8,128)})) %all-reduce.5.cloned.1.call-update) | async-done | bytes 1572880 | tf_op jit(solution)/shard_map/psum | solution.py:104
  419.4 2.3 slice_multiply_fusion
  421.7 0.8 broadcast_multiply_fusion
  (40 shorter events, 0.3 us)
Async XLA Ops:
  7.2 6.5 %copy-start = (bf16[2,6,128,128]{3,2,1,0:T(8,128)(2,1)S(1)}, bf16[2,6,128,128]{3,2,1,0:T(8,128)(2,1)}, u32[]{:S(2)}) copy-start(bf16[2,6,128,128]{3,2,1,0:T(8,128)(2,1)} %param.13) | copy-start | bytes 1179652
  8.1 0.6 copy-start.15
  8.8 4.9 %copy-start.9 = (s32[16,12]{0,1:T(8,128)}, s32[16,12]{0,1:T(8,128)S(1)}, u32[]{:S(2)}) copy-start(s32[16,12]{0,1:T(8,128)S(1)} %copy.74) | copy-start | bytes 2308
  10.6 3.1 copy-start.11
  12.7 1.0 copy-start.1
  25.2 11.4 %copy-start.13 = (bf16[1,2,256,256]{3,2,1,0:T(8,128)(2,1)S(1)}, bf16[1,2,256,256]{3,2,1,0:T(8,128)(2,1)}, u32[]{:S(2)}) copy-start(bf16[1,2,256,256]{3,2,1,0:T(8,128)(2,1)} %param.7) | copy-start | bytes 786436
  25.2 11.4 %copy-start.12 = (s32[16,12]{0,1:T(8,128)S(1)}, s32[16,12]{0,1:T(8,128)}, u32[]{:S(2)}) copy-start(s32[16,12]{0,1:T(8,128)} %copy-done.11) | copy-start | bytes 2308
  25.2 11.4 %copy-start.10 = (s32[16,12]{0,1:T(8,128)S(1)}, s32[16,12]{0,1:T(8,128)}, u32[]{:S(2)}) copy-start(s32[16,12]{0,1:T(8,128)} %copy-done.9) | copy-start | bytes 2308
  25.2 11.5 %copy-start.16 = (s32[16,12]{0,1:T(8,128)S(1)}, s32[16,12]{0,1:T(8,128)}, u32[]{:S(2)}) copy-start(s32[16,12]{0,1:T(8,128)} %get-tuple-element.19) | copy-start | bytes 2308
  25.2 11.7 %copy-start.5 = (bf16[2,256,256]{2,1,0:T(8,128)(2,1)S(1)}, bf16[2,256,256]{2,1,0:T(8,128)(2,1)}, u32[]{:S(2)}) copy-start(bf16[2,256,256]{2,1,0:T(8,128)(2,1)} %param.10) | copy-start | bytes 786436
  25.2 11.6 %copy-start.6 = (bf16[2,256,256]{2,1,0:T(8,128)(2,1)S(1)}, bf16[2,256,256]{2,1,0:T(8,128)(2,1)}, u32[]{:S(2)}) copy-start(bf16[2,256,256]{2,1,0:T(8,128)(2,1)} %param.9) | copy-start | bytes 786436
  25.2 60.2 %all-to-all-start = ((bf16[1,2,16,1,128,256]{5,4,1,3,0,2:T(8,128)(2,1)}), bf16[1,2,16,1,128,256]{5,4,1,3,0,2:T(8,128)(2,1)}, u32[]{:S(2)}, u32[]{:S(2)}) async-start(bf16[1,2,16,1,128,256]{5,4,1,3,0,2:T(8,128)(2,1)} %copy.82), calls=%async_computation | async-start | bytes 4194304 | tf_op jit(solution)/shard_map/all_to_all | solution.py:80
  36.3 98.9 %all-gather.2.cloned.1.call-start = ((), (), s32[]{:S(2)}) async-start(), calls=%async_computation.1 | async-start | bytes 4456448 | tf_op jit(solution)/shard_map/all_gather | solution.py:57
  36.9 0.7 copy-start.7
  38.9 49.3 %copy-start.17 = (pred[12]{0:T(512)(128)(4,1)S(1)}, pred[12]{0:T(512)(128)(4,1)}, u32[]{:S(2)}) copy-start(pred[12]{0:T(512)(128)(4,1)} %get-tuple-element.6) | copy-start | bytes 40
  88.2 1.2 copy-start.2
  89.5 1.8 copy-start.14
  90.5 328.8 %all-reduce.5.cloned.1.call-start = ((), (), s32[]{:S(2)}) async-start(), calls=%async_computation.2 | async-start | bytes 3145728 | tf_op jit(solution)/shard_map/psum | solution.py:104
  140.5 1.0 copy-start.3
  140.9 1.7 copy-start.8
  419.4 2.3 copy-start.4
Sparse Core Ops, SparseCore 0:
  90.6 44.5 all-gather.1
  142.7 276.6 all-reduce.4
where the time goes:
time: 430 us; the launch traced here: 429 us
  waiting for transfers between devices  364 us (85%)
  local copies, waits for them, and re-layouts  17 us (4%)
  matrix products  15.4 us (4%)
  between operations  14.3 us (3%)
  starting transfers between devices  11.2 us (3%)
  other arithmetic  6.99 us (2%)
    psum x1, waiting for transfers between devices, per_device(): conv_total, mix_total = lax.psum((conv_sum, mix_sum), ('dp', 'region'))  275 us
    all_to_all x1, waiting for transfers between devices, per_device(): lax.all_to_all(outgoing_back, 'region', split_axis=2, concat_axis=2, tile...  46.4 us
    all_gather x1, waiting for transfers between devices, per_device(): piece = lax.all_gather(tiled, 'region', axis=2, tiled=True)  42.5 us
    all_to_all x1, starting transfers between devices, per_device(): lax.all_to_all(outgoing_back, 'region', split_axis=2, concat_axis=2, tile...  11.1 us
  transfers between devices with their start and end apart: 3, of which 3 were waited for; matrix products, arithmetic and copies ran while one was open for 1% of the time, Pallas kernels for 0%

commit v1 on v0

--- a/solution.py
+++ b/solution.py
@@ -54,7 +54,9 @@
     gate = jax.nn.sigmoid(act[..., chans:])
     hidden = (filt * gate).astype(jnp.bfloat16)
     tiled = hidden.reshape(windows, steps, tiles_dev, 128, chans)
-    piece = lax.all_gather(tiled, "region", axis=2, tiled=True)
+    piece = jnp.concatenate(
+        lax.all_to_all(jnp.stack([tiled] * lax.axis_size("region")), "region", 0, 0), axis=2
+    )
     count = piece.shape[2]
     select = (own_tiles[:, None] == jnp.arange(count)[None, :]).astype(jnp.bfloat16)
     chosen = jnp.einsum("en,btnqc->bteqc", select, piece, preferred_element_type=jnp.float32)

time: 430 us -> 505 us (1.17)
  waiting for transfers between devices: 364 us -> 414 us
  local copies, waits for them, and re-layouts: 17 us -> 38.4 us
  starting transfers between devices: 11.2 us -> 16.4 us
    all_to_all x0 -> x1, waiting for transfers between devices: none -> 91.1 us  [per_device(): lax.all_to_all(jnp.stack([tiled] * lax.axis_size('region')), 'region', 0, 0)]
    all_gather x1 -> x0, waiting for transfers between devices: 42.5 us -> none  [per_device(): piece = lax.all_gather(tiled, 'region', axis=2, tiled=True)]
    another operation x0 -> x3, local copies, waits for them, and re-layouts: none -> 13.2 us
    reshape x1, local copies, waits for them, and re-layouts: 0.72 us -> 8.95 us  [per_device(): jnp.concatenate(lax.all_to_all(jnp.stack([tiled] * lax.axis_size('region'...]
    all_to_all x0 -> x1, starting transfers between devices: none -> 5.11 us  [per_device(): lax.all_to_all(jnp.stack([tiled] * lax.axis_size('region')), 'region', 0, 0)]
where the time goes in v1:
time: 505 us; the launch traced here: 504 us
  waiting for transfers between devices  414 us (82%)
  local copies, waits for them, and re-layouts  38.4 us (8%)
  starting transfers between devices  16.4 us (3%)
  between operations  14.3 us (3%)
  matrix products  13.8 us (3%)
  other arithmetic  6.99 us (1%)
    psum x1, waiting for transfers between devices, per_device(): conv_total, mix_total = lax.psum((conv_sum, mix_sum), ('dp', 'region'))  277 us
    all_to_all x1, waiting for transfers between devices, per_device(): lax.all_to_all(jnp.stack([tiled] * lax.axis_size('region')), 'region', 0, 0)  91.1 us
    all_to_all x1, waiting for transfers between devices, per_device(): lax.all_to_all(outgoing_back, 'region', split_axis=2, concat_axis=2, tile...  46.5 us
    all_to_all x1, starting transfers between devices, per_device(): lax.all_to_all(outgoing_back, 'region', split_axis=2, concat_axis=2, tile...  11.1 us
  transfers between devices with their start and end apart: 3, of which 3 were waited for; matrix products, arithmetic and copies ran while one was open for 1% of the time, Pallas kernels for 0%

profile of v1, /device:TPU:17, one launch (start us, length us, event | category | flops | bytes accessed | tf_op | source)
XLA Modules:
  0.0 504.2 jit_solution(12612671952381902416)
XLA Ops:
  7.2 0.8 copy.73
  8.0 0.1 reshape.360
  8.1 0.6 copy-done.15
  8.7 0.1 copy.74
  8.8 0.6 negate_select_fusion.4
  9.4 0.1 copy.78
  9.5 0.8 fusion.76
  10.2 0.4 convert_reduce_fusion
  10.6 0.2 select_reduce_fusion
  10.8 0.6 fusion.65
  11.4 1.4 convolution_bitcast_fusion
  12.8 0.9 copy-done.1
  13.7 0.6 fusion.7
  14.3 0.7 copy.80
  15.0 0.1 copy.81
  15.2 1.6 broadcast.248
  16.8 5.3 %scatter_fusion = bf16[2,16,128,256]{3,2,1,0:T(8,128)(2,1)} fusion(bf16[2,16,128,256]{3,2,1,0:T(8,128)(2,1)} %broadcast.248, s32[12]{0:T(128)} %fusion.65, bf16[12,2,128,256]{3,2,1,0:T(8,128)(2,1)S(1)} %copy.81), kind=kCustom, calls=%fused_computation | custom fusion | bytes 4718640 | tf_op jit(solution)/shard_map/scatter | solution.py:80
  22.1 3.1 copy.82
  25.2 11.1 %all-to-all-start = ((bf16[1,2,16,1,128,256]{5,4,1,3,0,2:T(8,128)(2,1)}), bf16[1,2,16,1,128,256]{5,4,1,3,0,2:T(8,128)(2,1)}, u32[]{:S(2)}, u32[]{:S(2)}) async-start(bf16[1,2,16,1,128,256]{5,4,1,3,0,2:T(8,128)(2,1)} %copy.82), calls=%async_computation | async-start | bytes 4194304 | tf_op jit(solution)/shard_map/all_to_all | solution.py:82
  36.3 0.1 reshape.365
  36.4 0.1 copy.85
  36.6 0.2 fusion.46
  36.9 0.6 copy-done.7
  37.5 1.4 convolution_bitcast_fusion.3
  38.9 46.5 %all-to-all-done = bf16[1,2,16,1,128,256]{5,4,1,3,0,2:T(8,128)(2,1)} async-done(((bf16[1,2,16,1,128,256]{5,4,1,3,0,2:T(8,128)(2,1)}), bf16[1,2,16,1,128,256]{5,4,1,3,0,2:T(8,128)(2,1)}, u32[]{:S(2)}, u32[]{:S(2)}) %all-to-all-start) | async-done | bytes 2097184 | tf_op jit(solution)/shard_map/all_to_all | solution.py:82
  85.4 2.9 fusion
  88.3 1.1 fusion.14
  89.4 0.1 copy-done.2
  89.5 0.3 fusion.37
  89.8 0.3 copy.92
  90.1 5.7 %stack.3 = bf16[16,1,2,2,128,256]{5,3,4,2,1,0:T(2,128)(2,1)} broadcast(bf16[2,2,128,256]{3,1,2,0:T(2,128)(2,1)S(1)} %copy.92), dimensions={2,3,4,5} | broadcast | bytes 4456448 | tf_op jit(solution)/shard_map/stack | solution.py:58
  95.8 5.1 %all-to-all-start.1 = ((bf16[16,1,2,2,128,256]{5,3,4,2,1,0:T(2,128)(2,1)}), bf16[16,1,2,2,128,256]{5,3,4,2,1,0:T(2,128)(2,1)}, u32[]{:S(2)}, u32[]{:S(2)}) async-start(bf16[16,1,2,2,128,256]{5,3,4,2,1,0:T(2,128)(2,1)} %stack.3), calls=%async_computation.1 | async-start | bytes 8388608 | tf_op jit(solution)/shard_map/all_to_all | solution.py:58
  100.9 0.2 all-reduce.5.cloned.1.call-start
  101.2 0.7 fusion.64
  101.9 1.5 convolution_bitcast_fusion.1
  103.4 91.1 %all-to-all-done.1 = bf16[16,1,2,2,128,256]{5,3,4,2,1,0:T(2,128)(2,1)} async-done(((bf16[16,1,2,2,128,256]{5,3,4,2,1,0:T(2,128)(2,1)}), bf16[16,1,2,2,128,256]{5,3,4,2,1,0:T(2,128)(2,1)}, u32[]{:S(2)}, u32[]{:S(2)}) %all-to-all-start.1) | async-done | bytes 4194336 | tf_op jit(solution)/shard_map/all_to_all | solution.py:58
  194.5 8.9 %copy.93 = bf16[1,2,16,2,128,256]{5,3,2,4,1,0:T(2,128)(2,1)} copy(bf16[1,2,16,2,128,256]{5,3,4,1,0,2:T(2,128)(2,1)} %bitcast.37) | data formatting | bytes 8388608 | tf_op jit(solution)/shard_map/reshape | solution.py:57
  203.5 7.2 %reshape.372 = bf16[2,32,128,256]{3,1,2,0:T(8,128)(2,1)} reshape(bf16[1,2,16,2,128,256]{5,3,2,4,1,0:T(2,128)(2,1)} %copy.93) | data formatting | bytes 8388608 | tf_op jit(solution)/shard_map/reshape.30
  210.7 2.9 convert_bitcast_fusion
  213.6 0.5 copy.94
  214.2 0.4 fusion.20
  214.6 0.5 copy-done.3
  215.1 1.1 convolution_bitcast_fusion.4
  216.3 0.5 convolution_bitcast_fusion.2
  216.8 0.8 fusion.27
  217.6 276.6 %all-reduce.5.cloned.1.call-done = (f32[512,512]{1,0:T(8,128)}, f32[512,256]{1,0:T(8,128)}) async-done(((f32[512,512]{1,0:T(8,128)}, f32[512,256]{1,0:T(8,128)}), (f32[512,512]{1,0:T(8,128)}, f32[512,256]{1,0:T(8,128)})) %all-reduce.5.cloned.1.call-update) | async-done | bytes 1572880 | tf_op jit(solution)/shard_map/psum | solution.py:106
  494.2 2.3 slice_multiply_fusion
  496.5 0.8 broadcast_multiply_fusion
  (42 shorter events, 0.3 us)
Async XLA Ops:
  7.2 6.5 %copy-start = (bf16[2,6,128,128]{3,2,1,0:T(8,128)(2,1)S(1)}, bf16[2,6,128,128]{3,2,1,0:T(8,128)(2,1)}, u32[]{:S(2)}) copy-start(bf16[2,6,128,128]{3,2,1,0:T(8,128)(2,1)} %param.13) | copy-start | bytes 1179652
  8.1 0.6 copy-start.15
  8.8 4.9 copy-start.9
  10.6 3.1 copy-start.11
  12.7 1.0 copy-start.1
  25.2 11.3 %copy-start.13 = (bf16[1,2,256,256]{3,2,1,0:T(8,128)(2,1)S(1)}, bf16[1,2,256,256]{3,2,1,0:T(8,128)(2,1)}, u32[]{:S(2)}) copy-start(bf16[1,2,256,256]{3,2,1,0:T(8,128)(2,1)} %param.7) | copy-start | bytes 786436
  25.2 11.3 %copy-start.12 = (s32[16,12]{0,1:T(8,128)S(1)}, s32[16,12]{0,1:T(8,128)}, u32[]{:S(2)}) copy-start(s32[16,12]{0,1:T(8,128)} %copy-done.11) | copy-start | bytes 2308
  25.2 11.4 %copy-start.10 = (s32[16,12]{0,1:T(8,128)S(1)}, s32[16,12]{0,1:T(8,128)}, u32[]{:S(2)}) copy-start(s32[16,12]{0,1:T(8,128)} %copy-done.9) | copy-start | bytes 2308
  25.2 11.4 %copy-start.16 = (s32[16,12]{0,1:T(8,128)S(1)}, s32[16,12]{0,1:T(8,128)}, u32[]{:S(2)}) copy-start(s32[16,12]{0,1:T(8,128)} %get-tuple-element.19) | copy-start | bytes 2308
  25.2 11.6 %copy-start.5 = (bf16[2,256,256]{2,1,0:T(8,128)(2,1)S(1)}, bf16[2,256,256]{2,1,0:T(8,128)(2,1)}, u32[]{:S(2)}) copy-start(bf16[2,256,256]{2,1,0:T(8,128)(2,1)} %param.10) | copy-start | bytes 786436
  25.2 11.6 %copy-start.6 = (bf16[2,256,256]{2,1,0:T(8,128)(2,1)S(1)}, bf16[2,256,256]{2,1,0:T(8,128)(2,1)}, u32[]{:S(2)}) copy-start(bf16[2,256,256]{2,1,0:T(8,128)(2,1)} %param.9) | copy-start | bytes 786436
  25.2 60.2 %all-to-all-start = ((bf16[1,2,16,1,128,256]{5,4,1,3,0,2:T(8,128)(2,1)}), bf16[1,2,16,1,128,256]{5,4,1,3,0,2:T(8,128)(2,1)}, u32[]{:S(2)}, u32[]{:S(2)}) async-start(bf16[1,2,16,1,128,256]{5,4,1,3,0,2:T(8,128)(2,1)} %copy.82), calls=%async_computation | async-start | bytes 4194304 | tf_op jit(solution)/shard_map/all_to_all | solution.py:82
  36.9 0.7 copy-start.7
  38.9 49.4 %copy-start.17 = (pred[12]{0:T(512)(128)(4,1)S(1)}, pred[12]{0:T(512)(128)(4,1)}, u32[]{:S(2)}) copy-start(pred[12]{0:T(512)(128)(4,1)} %get-tuple-element.6) | copy-start | bytes 40
  88.3 1.2 copy-start.2
  95.8 6.0 %copy-start.14 = (bf16[1,2,256,256]{3,2,1,0:T(8,128)(2,1)S(1)}, bf16[1,2,256,256]{3,2,1,0:T(8,128)(2,1)}, u32[]{:S(2)}) copy-start(bf16[1,2,256,256]{3,2,1,0:T(8,128)(2,1)} %param.7) | copy-start | bytes 786436
  95.8 98.7 %all-to-all-start.1 = ((bf16[16,1,2,2,128,256]{5,3,4,2,1,0:T(2,128)(2,1)}), bf16[16,1,2,2,128,256]{5,3,4,2,1,0:T(2,128)(2,1)}, u32[]{:S(2)}, u32[]{:S(2)}) async-start(bf16[16,1,2,2,128,256]{5,3,4,2,1,0:T(2,128)(2,1)} %stack.3), calls=%async_computation.1 | async-start | bytes 8388608 | tf_op jit(solution)/shard_map/all_to_all | solution.py:58
  100.9 393.3 %all-reduce.5.cloned.1.call-start = ((), (), s32[]{:S(2)}) async-start(), calls=%async_computation.2 | async-start | bytes 3145728 | tf_op jit(solution)/shard_map/psum | solution.py:106
  214.2 1.0 copy-start.3
  214.6 1.7 copy-start.8
  494.2 2.3 copy-start.4
Sparse Core Ops, SparseCore 0:
  216.4 277.7 all-reduce.4
